TPU v7x, 256 devices: a whole 4x4x8 slice. The times are simulated.
256 devices in a mesh: ctx: 64 (over z, x, y_lo), dp: 4 (over y_hi, core).
Axes of the slice: x: 4, y: 4 (y_hi: 2, y_lo: 2; y = y_hi * 2 + y_lo), z: 8, core: 2. Of those that a mesh axis runs over, the one named last changes fastest.
Arguments:
- queries: bfloat16 [8192, 4096], P('ctx', 'dp'), may hold values from -100 to 100
- keys: bfloat16 [8192, 512], P('ctx', 'dp'), may hold values from -15 to 15
- values: bfloat16 [8192, 512], P('ctx', 'dp'), may hold values from -6 to 6
- segment_ids: int32 [8192], P('ctx'), may hold values from 0 to 3, never falling along the last dimension, each value on 1 to 4096 neighbouring positions
- cart_keys: bfloat16 [1024, 512], P('ctx', 'dp'), may hold values from -12 to 12
- cart_values: bfloat16 [1024, 512], P('ctx', 'dp'), may hold values from -6 to 6
Outputs:
- teacher_out: bfloat16 [8192, 4096], P('ctx', 'dp')
- student_out: bfloat16 [8192, 4096], P('ctx', 'dp')
- grad_keys: float32 [1024, 512], P('ctx')
- grad_values: float32 [1024, 512], P('ctx')
Inputs may be any that keep to these rules, and one draw needn't show every extreme that they name: `segment_ids`: document numbers never fall along the context; each document spans 1 to 4096 positions, one exactly that many.
All inputs are finite; a program needn't handle non-finite values.
Results may differ from a plain program's by a relative error of at most 0.0085.
The roundings to bfloat16 on the way count: a program that leaves them out, or rounds other values in their place, can miss the bound.
Values may be sent and summed in bfloat16 or wider, within the bound.
A program may use at most 64 MiB of HBM per device.

v0:
```python
import math
import jax
import jax.numpy as jnp
from jax import lax
from jax.sharding import PartitionSpec as P

HQ = 32
KVH = 4
HD = 128
distill_weight = 8.0
masked_score = -1e30


def per_device(queries, keys, values, segment_ids, cart_keys, cart_values):
    row_count = queries.shape[0]
    query_width = queries.shape[1]
    kv_local = keys.shape[1] // HD
    group_size = HQ // KVH
    score_scale = 1.0 / math.sqrt(HD)
    position = lax.axis_index("ctx")
    first_row = position * row_count
    last_row = first_row + row_count - 1
    query_heads = queries.reshape(row_count, kv_local, group_size, HD)
    query_pos = first_row + jnp.arange(row_count, dtype=jnp.int32)
    query_seg = segment_ids.astype(jnp.bfloat16)

    def attend(state, key_start, key_block, value_block, seg_block):
        running_max, running_sum, running_out = state
        width = key_block.shape[0]
        key_heads = key_block.reshape(width, kv_local, HD)
        value_heads = value_block.reshape(width, kv_local, HD)
        scores = (
            jnp.einsum("ikgd,jkd->kgij", query_heads, key_heads, preferred_element_type=jnp.float32)
            * score_scale
        )
        key_pos = key_start + jnp.arange(width, dtype=jnp.int32)
        allowed = (key_pos[None, :] <= query_pos[:, None]) & (
            seg_block[None, :] == query_seg[:, None]
        )
        scores = jnp.where(allowed[None, None], scores, masked_score)
        new_max = jnp.maximum(running_max, jnp.max(scores, axis=-1))
        factor = jnp.exp(running_max - new_max)
        weights = jnp.exp(scores - new_max[..., None])
        running_sum = running_sum * factor + jnp.sum(weights, axis=-1)
        running_out = running_out * factor[..., None] + jnp.einsum(
            "kgij,jkd->kgid",
            weights.astype(jnp.bfloat16),
            value_heads,
            preferred_element_type=jnp.float32,
        )
        return (new_max, running_sum, running_out)

    state = (
        jnp.full((kv_local, group_size, row_count), masked_score, jnp.float32),
        jnp.zeros((kv_local, group_size, row_count), jnp.float32),
        jnp.zeros((kv_local, group_size, row_count, HD), jnp.float32),
    )
    current = state
    key_piece = lax.all_gather(keys, "ctx", axis=0, tiled=True)
    value_piece = lax.all_gather(values, "ctx", axis=0, tiled=True)
    seg_piece = lax.all_gather(query_seg, "ctx", axis=0, tiled=True)
    width = min(row_count, key_piece.shape[0])
    count = key_piece.shape[0] // width

    def visit(inner, inputs):
        index, key_block, value_block, seg_block = inputs
        key_start = index * width
        inner = lax.cond(
            key_start <= last_row,
            lambda held: attend(held, key_start, key_block, value_block, seg_block),
            lambda held: held,
            inner,
        )
        return (inner, None)

    current, unused = lax.scan(
        visit,
        current,
        (
            jnp.arange(count, dtype=jnp.int32),
            key_piece.reshape(count, width, key_piece.shape[1]),
            value_piece.reshape(count, width, value_piece.shape[1]),
            seg_piece.reshape(count, width),
        ),
    )
    state = current
    running_max, running_sum, running_out = state
    teacher_heads = running_out / running_sum[..., None]
    teacher_rows = (
        jnp.transpose(teacher_heads, (2, 0, 1, 3))
        .reshape(row_count, query_width)
        .astype(jnp.bfloat16)
    )
    slot_keys, slot_values = (
        lax.all_gather(cart_keys, "ctx", axis=0, tiled=True),
        lax.all_gather(cart_values, "ctx", axis=0, tiled=True),
    )
    slot_count = slot_keys.shape[0]
    slot_key_heads = slot_keys.reshape(slot_count, kv_local, HD)
    slot_value_heads = slot_values.reshape(slot_count, kv_local, HD)
    target = teacher_rows.reshape(row_count, kv_local, group_size, HD)
    head_query = query_heads[:, 0]
    head_keys = slot_key_heads[:, 0]
    head_values = slot_value_heads[:, 0]
    logits = (
        jnp.einsum("igd,sd->gis", head_query, head_keys, preferred_element_type=jnp.float32)
        * score_scale
    )
    probs = jax.nn.softmax(logits, axis=-1)
    probs_low = probs.astype(jnp.bfloat16)
    student = jnp.einsum("gis,sd->igd", probs_low, head_values, preferred_element_type=jnp.float32)
    delta = (distill_weight * (student - target[:, 0].astype(jnp.float32))).astype(jnp.bfloat16)
    back = jnp.einsum("igd,sd->gis", delta, head_values, preferred_element_type=jnp.float32)
    row_term = jnp.einsum("igd,igd->gi", delta.astype(jnp.float32), student)
    score_grad = (probs * (back - row_term[..., None])).astype(jnp.bfloat16)
    value_grads = [jnp.einsum("gis,igd->sd", probs_low, delta, preferred_element_type=jnp.float32)]
    key_grads = [
        jnp.einsum("gis,igd->sd", score_grad, head_query, preferred_element_type=jnp.float32)
        * score_scale
    ]
    student_list = [student.astype(jnp.bfloat16)]
    student_rows = jnp.stack(student_list, axis=1).reshape(row_count, query_width)
    relaid = lax.all_to_all(student_rows, "ctx", split_axis=0, concat_axis=0, tiled=True)
    local_width = kv_local * HD
    grads = jnp.concatenate(
        [
            jnp.stack(key_grads, axis=1).reshape(slot_count, local_width),
            jnp.stack(value_grads, axis=1).reshape(slot_count, local_width),
        ],
        axis=1,
    )
    summed = lax.psum(grads, "ctx")
    share = slot_count // lax.axis_size("ctx")
    owned = lax.dynamic_slice_in_dim(summed, lax.axis_index("ctx") * share, share, 0)
    key_full, value_full = (
        lax.all_gather(owned[:, :local_width], "dp", axis=1, tiled=True),
        lax.all_gather(owned[:, local_width:], "dp", axis=1, tiled=True),
    )
    return (teacher_rows, relaid, key_full, value_full)


def solution(mesh):
    in_specs = (
        P("ctx", "dp"),
        P("ctx", "dp"),
        P("ctx", "dp"),
        P("ctx"),
        P("ctx", "dp"),
        P("ctx", "dp"),
    )
    out_specs = (P("ctx", "dp"), P("ctx", "dp"), P("ctx", None), P("ctx", None))
    return jax.shard_map(
        per_device, mesh=mesh, in_specs=in_specs, out_specs=out_specs, check_vma=False
    )
```

profile of v0, /device:TPU:1, one launch (start us, length us, event | category | flops | bytes accessed | tf_op | source)
XLA Modules:
  0.0 1500.4 jit_solution(12708167369714326601)
XLA Ops:
  9.4 132.1 %all-gather = bf16[64,1,128]{2,1,0:T(2,128)(2,1)S(1)} all-gather(bf16[1,1,128]{2,1,0:T(2,128)(2,1)S(1)} %get-tuple-element.277), channel_id=1, replica_groups=mesh['ctx'=64,'dp'=4] {'ctx'}, dimensions={0}, use_global_device_ids=true | all-gather | bytes 16640 | tf_op jit(solution)/shard_map/all_gather | solution.py:61
  141.5 1.1 copy.34
  142.8 126.1 %all_gather.25 = bf16[1024,128]{1,0:T(8,128)(2,1)S(1)} all-gather(bf16[16,128]{1,0:T(8,128)(2,1)} %param.15), channel_id=1, replica_groups=mesh['ctx'=64,'dp'=4] {'ctx'}, dimensions={0}, use_global_device_ids=true | all-gather | bytes 266240 | tf_op jit(solution)/shard_map/all_gather | solution.py:96
  268.8 126.9 %all_gather.24 = bf16[1024,128]{1,0:T(8,128)(2,1)S(1)} all-gather(bf16[16,128]{1,0:T(8,128)(2,1)} %param.14), channel_id=1, replica_groups=mesh['ctx'=64,'dp'=4] {'ctx'}, dimensions={0}, use_global_device_ids=true | all-gather | bytes 266240 | tf_op jit(solution)/shard_map/all_gather | solution.py:95
  395.7 3.3 fusion.55
  399.0 2.5 fusion.28
  401.6 163.9 %all-gather.6.cloned.1.call-done = bf16[8192,128]{1,0:T(8,128)(2,1)} async-done(((bf16[128,128]{1,0:T(8,128)(2,1)}), bf16[8192,128]{1,0:T(8,128)(2,1)}) %all-gather.6.cloned.1.call-update) | async-done | bytes 2097168 | tf_op jit(solution)/shard_map/all_gather | solution.py:60
  565.6 91.0 %while.15 = (s32[]{:T(128)}, f32[1,8,128]{2,1,0:T(8,128)S(1)}, f32[1,8,128]{2,1,0:T(8,128)S(1)}, f32[1,8,128,128]{3,2,1,0:T(8,128)S(1)}, s32[64]{0:T(128)S(1)}, ...) while((s32[]{:T(128)}, f32[1,8,128]{2,1,0:T(8,128)S(1)}, ...), condition=%wide.region_5.6_spmd.clone, body=%wide.region_0.5_spmd.clone.sunk | while | flops 68373760 | bytes 3052887 | solution.py:76
  567.0 2.5 conditional.3
  567.1 1.0 fusion.52
  568.2 1.2 fusion.3
  656.6 1.6 fusion.34
  658.2 0.8 convolution_bitcast_fusion.1
  659.0 3.7 fusion.31
  662.8 1.1 pad_maximum_fusion
  664.1 0.8 all_to_all.8
  664.9 162.9 %all-to-all-start = ((bf16[64,2,1024]{2,1,0:T(2,128)(2,1)}), bf16[64,2,1024]{2,1,0:T(2,128)(2,1)S(1)}, u32[]{:S(2)}, u32[]{:S(2)}) async-start(bf16[64,2,1024]{2,1,0:T(2,128)(2,1)} %all_to_all.8), calls=%async_computation | async-start | bytes 524288 | tf_op jit(solution)/shard_map/all_to_all | solution.py:123
  828.0 0.9 copy.45
  828.8 9.6 all-to-all-done
  838.4 0.8 all_to_all.10
  839.2 593.9 %all-reduce.2.cloned.1.call-done = f32[1024,256]{0,1:T(8,128)} async-done(((f32[1024,256]{0,1:T(8,128)}), f32[1024,256]{0,1:T(8,128)}) %all-reduce.2.cloned.1.call-update) | async-done | bytes 1048592 | tf_op jit(solution)/shard_map/psum | solution.py:132
  1433.1 1.0 fusion.53
  1434.0 51.0 %all_gather.27 = f32[16,512]{0,1:T(8,128)S(1)} all-gather(f32[16,128]{0,1:T(8,128)S(1)} %get-tuple-element.273), channel_id=1, replica_groups=mesh['ctx'=64,'dp'=4] {'dp'}, dimensions={1}, use_global_device_ids=true | all-gather | bytes 40960 | tf_op jit(solution)/shard_map/all_gather | solution.py:137
  1485.8 7.3 all_gather.26
  (220 shorter events, 47.0 us)
Async XLA Ops:
  7.2 394.5 %all-gather.4.cloned.1.call-start = ((), (), s32[]{:S(2)}) async-start(), calls=%async_computation.1 | async-start | bytes 2129920 | tf_op jit(solution)/shard_map/all_gather | solution.py:59
  7.9 557.7 %all-gather.6.cloned.1.call-start = ((), (), s32[]{:S(2)}) async-start(), calls=%async_computation.2 | async-start | bytes 2129920 | tf_op jit(solution)/shard_map/all_gather | solution.py:60
  8.6 1424.4 %all-reduce.2.cloned.1.call-start = ((), (), s32[]{:S(2)}) async-start(), calls=%async_computation.3 | async-start | bytes 2097152 | tf_op jit(solution)/shard_map/psum | solution.py:132
  658.2 0.8 copy-start
  659.0 4.9 copy-start.1
  664.9 173.5 %all-to-all-start = ((bf16[64,2,1024]{2,1,0:T(2,128)(2,1)}), bf16[64,2,1024]{2,1,0:T(2,128)(2,1)S(1)}, u32[]{:S(2)}, u32[]{:S(2)}) async-start(bf16[64,2,1024]{2,1,0:T(2,128)(2,1)} %all_to_all.8), calls=%async_computation | async-start | bytes 524288 | tf_op jit(solution)/shard_map/all_to_all | solution.py:123
Sparse Core Ops, SparseCore 0:
  9.8 256.8 all-gather.3
  268.4 297.0 all-gather.5
  664.1 768.9 all-reduce.1
where the time goes:
time: 1510 us; the launch traced here: 1500 us
  waiting for transfers between devices  769 us (51%)
  blocking collectives  443 us (29%)
  starting transfers between devices  163 us (11%)
  local copies, waits for them, and re-layouts  48.3 us (3%)
  loops' own time  46.9 us (3%)
    psum x1, waiting for transfers between devices, per_device(): summed = lax.psum(grads, 'ctx')  594 us
    all_gather x1, waiting for transfers between devices, per_device(): value_piece = lax.all_gather(values, 'ctx', axis=0, tiled=True)  164 us
    all_to_all x1, starting transfers between devices, per_device(): lax.all_to_all(student_rows, 'ctx', split_axis=0, concat_axis=0, tiled=True)  163 us
    all_gather x1, blocking collectives, per_device(): seg_piece = lax.all_gather(query_seg, 'ctx', axis=0, tiled=True)  132 us
    all_gather x1, blocking collectives, per_device(): lax.all_gather(cart_keys, 'ctx', axis=0, tiled=True)  127 us
    all_gather x1, blocking collectives, per_device(): lax.all_gather(cart_values, 'ctx', axis=0, tiled=True)  126 us
    all_gather x1, blocking collectives, per_device(): lax.all_gather(owned[:, local_width:], 'dp', axis=1, tiled=True)  51 us
    another operation x1, loops' own time, per_device(): lax.scan(visit, current, (jnp.arange(count, dtype=jnp.int32), key_piece.r...  45.9 us
  transfers between devices with their start and end apart: 4, of which 3 were waited for; matrix products, arithmetic and copies ran while one was open for 1% of the time, Pallas kernels for 0%

commit v1 on v0

--- a/solution.py
+++ b/solution.py
@@ -56,8 +56,11 @@
         jnp.zeros((kv_local, group_size, row_count, HD), jnp.float32),
     )
     current = state
-    key_piece = lax.all_gather(keys, "ctx", axis=0, tiled=True)
-    value_piece = lax.all_gather(values, "ctx", axis=0, tiled=True)
+    key_piece, value_piece = jnp.split(
+        lax.all_gather(jnp.concatenate([keys, values], axis=1), "ctx", axis=0, tiled=True),
+        [keys.shape[1]],
+        axis=1,
+    )
     seg_piece = lax.all_gather(query_seg, "ctx", axis=0, tiled=True)
     width = min(row_count, key_piece.shape[0])
     count = key_piece.shape[0] // width

time: 1510 us -> 1390 us (0.921)
  waiting for transfers between devices: 769 us -> 637 us
    all_gather x2 -> x1, waiting for transfers between devices: 164 us -> 0.02 us  [per_device(): lax.all_gather(jnp.concatenate([keys, values], axis=1), 'ctx', axis=0, ti...]
    all_gather x1, blocking collectives: 51 us -> 7.34 us  [per_device(): lax.all_gather(owned[:, local_width:], 'dp', axis=1, tiled=True)]
    all_gather x1, blocking collectives: 7.34 us -> 51 us  [per_device(): lax.all_gather(owned[:, :local_width], 'dp', axis=1, tiled=True)]
    psum x1, waiting for transfers between devices: 594 us -> 627 us  [per_device(): summed = lax.psum(grads, 'ctx')]
  transfers between devices with their start and end apart: 4 -> 3, of which waited for: 3 -> 2; matrix products, arithmetic and copies ran while one was open for 1% -> 1% of each run, Pallas kernels for 0% -> 0%
where the time goes in v1:
time: 1390 us; the launch traced here: 1380 us
  waiting for transfers between devices  637 us (46%)
  blocking collectives  454 us (33%)
  starting transfers between devices  159 us (11%)
  local copies, waits for them, and re-layouts  48.7 us (4%)
  loops' own time  44.9 us (3%)
  between operations  14.2 us (1%)
    psum x1, waiting for transfers between devices, per_device(): summed = lax.psum(grads, 'ctx')  627 us
    all_to_all x1, starting transfers between devices, per_device(): lax.all_to_all(student_rows, 'ctx', split_axis=0, concat_axis=0, tiled=True)  159 us
    all_gather x1, blocking collectives, per_device(): lax.all_gather(cart_values, 'ctx', axis=0, tiled=True)  136 us
    all_gather x1, blocking collectives, per_device(): seg_piece = lax.all_gather(query_seg, 'ctx', axis=0, tiled=True)  133 us
    all_gather x1, blocking collectives, per_device(): lax.all_gather(cart_keys, 'ctx', axis=0, tiled=True)  127 us
    all_gather x1, blocking collectives, per_device(): lax.all_gather(owned[:, :local_width], 'dp', axis=1, tiled=True)  51 us
    another operation x1, loops' own time, per_device(): lax.scan(visit, current, (jnp.arange(count, dtype=jnp.int32), key_piece.r...  44.1 us
    dynamic_slice x65, local copies, waits for them, and re-layouts, per_device(): lax.scan(visit, current, (jnp.arange(count, dtype=jnp.int32), key_piece.r...  37.6 us
  transfers between devices with their start and end apart: 3, of which 2 were waited for; matrix products, arithmetic and copies ran while one was open for 1% of the time, Pallas kernels for 0%

profile of v1, /device:TPU:1, one launch (start us, length us, event | category | flops | bytes accessed | tf_op | source)
XLA Modules:
  0.0 1375.8 jit_solution(9802321759993477726)
XLA Ops:
  7.2 1.4 pad_maximum_fusion.1
  8.7 1.1 copy.34
  10.7 132.6 %all-gather = bf16[64,1,128]{2,1,0:T(2,128)(2,1)S(1)} all-gather(bf16[1,1,128]{2,1,0:T(2,128)(2,1)S(1)} %get-tuple-element.279), channel_id=1, replica_groups=mesh['ctx'=64,'dp'=4] {'ctx'}, dimensions={0}, use_global_device_ids=true | all-gather | bytes 16640 | tf_op jit(solution)/shard_map/all_gather | solution.py:64
  143.3 126.5 %all_gather.20 = bf16[1024,128]{1,0:T(8,128)(2,1)S(1)} all-gather(bf16[16,128]{1,0:T(8,128)(2,1)} %param.14), channel_id=1, replica_groups=mesh['ctx'=64,'dp'=4] {'ctx'}, dimensions={0}, use_global_device_ids=true | all-gather | bytes 266240 | tf_op jit(solution)/shard_map/all_gather | solution.py:98
  269.8 136.1 %all_gather.21 = bf16[1024,128]{1,0:T(8,128)(2,1)} all-gather(bf16[16,128]{1,0:T(8,128)(2,1)} %param.15), channel_id=1, replica_groups=mesh['ctx'=64,'dp'=4] {'ctx'}, dimensions={0}, use_global_device_ids=true | all-gather | bytes 266240 | tf_op jit(solution)/shard_map/all_gather | solution.py:99
  405.9 3.3 fusion.56
  409.2 2.5 fusion.28
  411.8 4.4 fusion.53
  416.3 85.0 %while.15 = (s32[]{:T(128)}, f32[1,8,128]{2,1,0:T(8,128)S(1)}, f32[1,8,128]{2,1,0:T(8,128)S(1)}, f32[1,8,128,128]{3,2,1,0:T(8,128)S(1)}, s32[64]{0:T(128)S(1)}, ...) while((s32[]{:T(128)}, f32[1,8,128]{2,1,0:T(8,128)S(1)}, ...), condition=%wide.region_5.6_spmd.clone, body=%wide.region_0.5_spmd.clone.sunk | while | flops 68373760 | bytes 3052879 | solution.py:79
  417.6 2.5 conditional.3
  417.7 1.0 fusion.52
  418.7 1.2 fusion.3
  501.3 2.5 fusion.34
  503.8 0.8 convolution_bitcast_fusion.1
  504.7 3.8 fusion.31
  508.5 1.1 pad_maximum_fusion
  510.6 158.9 %all-to-all-start = ((bf16[64,2,1024]{2,1,0:T(2,128)(2,1)}), bf16[64,2,1024]{2,1,0:T(2,128)(2,1)S(1)}, u32[]{:S(2)}, u32[]{:S(2)}) async-start(bf16[64,2,1024]{2,1,0:T(2,128)(2,1)} %all_to_all.8), calls=%async_computation | async-start | bytes 524288 | tf_op jit(solution)/shard_map/all_to_all | solution.py:126
  669.7 0.9 copy.45
  670.5 9.6 all-to-all-done
  680.1 0.8 all_to_all.10
  680.9 627.2 %all-reduce.2.cloned.1.call-done = f32[1024,256]{0,1:T(8,128)} async-done(((f32[1024,256]{0,1:T(8,128)}), f32[1024,256]{0,1:T(8,128)}) %all-reduce.2.cloned.1.call-update) | async-done | bytes 1048592 | tf_op jit(solution)/shard_map/psum | solution.py:135
  1308.1 1.0 fusion.54
  1309.1 51.0 %all_gather.22 = f32[16,512]{0,1:T(8,128)S(1)} all-gather(f32[16,128]{0,1:T(8,128)S(1)} %get-tuple-element.276), channel_id=1, replica_groups=mesh['ctx'=64,'dp'=4] {'dp'}, dimensions={1}, use_global_device_ids=true | all-gather | bytes 40960 | tf_op jit(solution)/shard_map/all_gather | solution.py:139
  1360.9 7.3 all_gather.23
  (219 shorter events, 42.2 us)
Async XLA Ops:
  7.2 404.6 %all-gather.3.cloned.1.call-start = ((), (), s32[]{:S(2)}) async-start(), calls=%async_computation.1 | async-start | bytes 4259840 | tf_op jit(solution)/shard_map/all_gather | solution.py:60
  8.6 1299.5 %all-reduce.2.cloned.1.call-start = ((), (), s32[]{:S(2)}) async-start(), calls=%async_computation.2 | async-start | bytes 2097152 | tf_op jit(solution)/shard_map/psum | solution.py:135
  503.8 0.8 copy-start
  504.7 5.0 copy-start.1
  510.6 169.5 %all-to-all-start = ((bf16[64,2,1024]{2,1,0:T(2,128)(2,1)}), bf16[64,2,1024]{2,1,0:T(2,128)(2,1)S(1)}, u32[]{:S(2)}, u32[]{:S(2)}) async-start(bf16[64,2,1024]{2,1,0:T(2,128)(2,1)} %all_to_all.8), calls=%async_computation | async-start | bytes 524288 | tf_op jit(solution)/shard_map/all_to_all | solution.py:126
Sparse Core Ops, SparseCore 0:
  10.3 261.3 all-gather.2
  509.7 798.3 all-reduce.1
